TPU v7x, 32 devices: a whole 2x2x4 slice. The times are simulated.
32 devices in a mesh: ctx: 16 (over z, y, x), head: 2 (over core).
Axes of the slice: x: 2, y: 2, z: 4, core: 2. Of those that a mesh axis runs over, the one named last changes fastest.
Arguments:
- queries: bfloat16 [2, 4096, 2048], P(None, 'ctx', 'head'), may hold values from -6 to 6
- key_vectors: bfloat16 [2, 4096, 2048], P(None, 'ctx', 'head'), may hold values from -0.4 to 0.4
- value_vectors: bfloat16 [2, 4096, 2048], P(None, 'ctx', 'head'), may hold values from -6 to 6
- log_decay: float32 [16, 2, 4096], P('head', None, 'ctx'), may hold values from -1 to 0
- ridge_shift: float32 [16], P('head'), may hold values from 0.25 to 4
- norm_gain: float32 [2048], P('head'), may hold values from 0.1 to 1.9
- out_weight: bfloat16 [2048, 4096], P(None, 'head'), may hold values from -0.125 to 0.125
Outputs:
- mixed: bfloat16 [2, 4096, 4096], P(None, 'ctx', 'head')
All inputs are finite; a program needn't handle non-finite values.
Results may differ from a plain program's by a relative error of at most 0.007.
Values may be sent and summed in bfloat16 or wider, within the bound.
No kernel may reach another device: no remote copies, remote signals or barrier semaphores. Data moves between devices by JAX's collectives and lax.ppermute only.
A program may use at most 128 MiB of HBM per device.

v0:
```python
import jax
import jax.numpy as jnp
from jax import lax
from jax.sharding import PartitionSpec as P

DK = 128
DV = 128
GROUP = 256
ITERS = 2
exact_mode = lax.Precision.HIGHEST
norm_epsilon = 1e-06
solve_epsilon = 1e-06


def entering_2(value, axis, join, neutral):
    count, mine = (lax.axis_size(axis), lax.axis_index(axis))
    pieces = jax.tree.map(lambda part: lax.all_gather(part, axis), value)
    total = jax.tree.map(
        lambda part, zero: jnp.full_like(part, 0) + jnp.asarray(zero, part.dtype), value, neutral
    )

    def lap(position, total):
        longer = join(total, jax.tree.map(lambda part: part[position], pieces))
        return jax.tree.map(lambda new, old: jnp.where(position < mine, new, old), longer, total)

    return lax.fori_loop(0, count - 1, lap, total)


def for_sending(shard):
    return jax.tree.map(lambda a: a.astype(jnp.bfloat16) if a.dtype == jnp.float32 else a, shard)


def broadcast(shard, axis, root):
    mine = lax.axis_index(axis) == root
    return lax.psum(jnp.where(mine, shard, jnp.zeros_like(shard)), axis)


def carried_in(shard, axis, join, neutral):
    count = lax.axis_size(axis)
    place = lax.axis_index(axis)
    ahead = count - 1 - place
    gathered = jax.tree.map(
        lambda a, kind: lax.all_gather(a.astype(kind), axis),
        shard,
        jax.tree.map(lambda a: jnp.bfloat16 if a.dtype == jnp.float32 else a.dtype, shard),
    )
    state = jax.tree.map(lambda a, e: jnp.zeros_like(a) + jnp.asarray(e, a.dtype), shard, neutral)

    def one(lap, state):
        source = count - 1 - lap
        return join(
            state,
            jax.tree.map(
                lambda a, own: lax.dynamic_index_in_dim(a, source, 0, False).astype(own.dtype),
                gathered,
                shard,
            ),
        )

    return lax.fori_loop(0, ahead, one, state)


def decay_masks(log_rates):
    cumulative = jnp.cumsum(log_rates, axis=-1)
    width_now = log_rates.shape[-1]
    differ = cumulative[..., :, None] - cumulative[..., None, :]
    lower_part = jnp.arange(width_now)[:, None] >= jnp.arange(width_now)[None, :]
    within = jnp.where(lower_part, jnp.exp(jnp.minimum(differ, 0.0)), 0.0)
    return (cumulative, within)


def group_state(key_rows, value_rows, cumulative):
    weights = jnp.exp(cumulative[..., -1:] - cumulative)[..., None]
    key_gram = jnp.einsum("...sd,...se->...de", key_rows * weights, key_rows, precision=exact_mode)
    value_key = jnp.einsum(
        "...se,...sd->...ed", value_rows * weights, key_rows, precision=exact_mode
    )
    return (cumulative[..., -1], key_gram, value_key)


def group_outputs(
    query_rows, key_rows, value_rows, cumulative, within, key_gram, value_key, ridge_term
):
    entering = jnp.exp(cumulative)[..., None]
    solution = jnp.zeros_like(query_rows)
    residual = query_rows
    direction = query_rows
    norm_now = jnp.sum(residual * residual, axis=-1, keepdims=True)
    for iteration in range(ITERS):
        operator_scores = (
            jnp.einsum("...cd,...sd->...cs", direction, key_rows, precision=exact_mode) * within
        )
        operator_carried = jnp.einsum(
            "...cd,...de->...ce", direction, key_gram, precision=exact_mode
        )
        local_part = jnp.einsum(
            "...cs,...sd->...cd", operator_scores, key_rows, precision=exact_mode
        )
        product = entering * operator_carried + local_part + ridge_term * direction
        step_size = norm_now / (
            jnp.sum(direction * product, axis=-1, keepdims=True) + solve_epsilon
        )
        solution = solution + step_size * direction
        residual = residual - step_size * product
        if iteration + 1 < ITERS:
            norm_next = jnp.sum(residual * residual, axis=-1, keepdims=True)
            direction = residual + norm_next / (norm_now + solve_epsilon) * direction
            norm_now = norm_next
    scores = jnp.einsum("...cd,...sd->...cs", solution, key_rows, precision=exact_mode) * within
    carried = jnp.einsum("...cd,...ed->...ce", solution, value_key, precision=exact_mode)
    return entering * carried + jnp.einsum(
        "...cs,...se->...ce", scores, value_rows, precision=exact_mode
    )


def finish(readout, gain_rows):
    scale_rows = lax.rsqrt(jnp.mean(readout * readout, axis=-1, keepdims=True) + norm_epsilon)
    return (readout * scale_rows * gain_rows).astype(jnp.bfloat16)


def combine(earlier, latter):
    fading = jnp.exp(latter[0])[..., None, None]
    return (
        earlier[0] + latter[0],
        fading * earlier[1] + latter[1],
        fading * earlier[2] + latter[2],
    )


def on_device(queries, key_vectors, value_vectors, log_decay, ridge_shift, norm_gain, out_weight):
    block_len = queries.shape[1]
    local_heads = queries.shape[2] // DK
    group_count = block_len // GROUP

    def split_heads(packed, feature_width):
        return (
            packed.astype(jnp.float32)
            .reshape(2, group_count, GROUP, local_heads, feature_width)
            .transpose(0, 3, 1, 2, 4)
        )

    query_rows = split_heads(queries, DK)
    key_rows = split_heads(key_vectors, DK)
    value_rows = split_heads(value_vectors, DV)
    log_rates = log_decay.reshape(local_heads, 2, group_count, GROUP).transpose(1, 0, 2, 3)
    cumulative, within = decay_masks(log_rates)
    totals, key_grams, value_keys = group_state(key_rows, value_rows, cumulative)
    running = (
        jnp.zeros_like(totals[:, :, 0]),
        jnp.zeros_like(key_grams[:, :, 0]),
        jnp.zeros_like(value_keys[:, :, 0]),
    )
    prefixes = []
    prefixes.append(running)
    running = combine(running, (totals[:, :, 0], key_grams[:, :, 0], value_keys[:, :, 0]))
    first = tuple((member[0] for member in running))
    second = tuple((member[1] for member in running))
    neutral = tuple((jnp.zeros_like(member) for member in first))
    ridge_term = ridge_shift[:, None, None, None]
    gain_rows = norm_gain.reshape(local_heads, 1, 1, DV)

    def solve_row(half_row, entering):
        entering_group = combine(entering, tuple((member[half_row] for member in prefixes[0])))
        gram_list = [entering_group[1]]
        memory_list = [entering_group[2]]
        key_gram = jnp.stack(gram_list, axis=1)
        value_key = jnp.stack(memory_list, axis=1)
        readout = group_outputs(
            query_rows[half_row],
            key_rows[half_row],
            value_rows[half_row],
            cumulative[half_row],
            within[half_row],
            key_gram,
            value_key,
            ridge_term,
        )
        normed = finish(readout, gain_rows)
        return normed.transpose(1, 2, 0, 3).reshape(block_len, local_heads * DV)

    before = entering_2(first, "ctx", combine, neutral)
    front_rows = solve_row(0, before)
    whole_first = jax.tree.map(
        lambda part: broadcast(part, "ctx", lax.axis_size("ctx") - 1),
        for_sending(combine(before, first)),
    )
    from_later = carried_in(second, "ctx", combine, neutral)
    entering_second = combine(whole_first, from_later)
    back_rows = solve_row(1, entering_second)
    flattened = jnp.concatenate([front_rows, back_rows], axis=0)
    columns = out_weight.shape[1]
    mixed_out = jnp.dot(
        lax.all_gather(flattened, "head", axis=1, tiled=True),
        out_weight,
        preferred_element_type=jnp.float32,
    )
    return mixed_out.astype(jnp.bfloat16).reshape(2, block_len, columns)


def solution(mesh):
    return jax.shard_map(
        on_device,
        mesh=mesh,
        in_specs=(
            P(None, "ctx", "head"),
            P(None, "ctx", "head"),
            P(None, "ctx", "head"),
            P("head", None, "ctx"),
            P("head"),
            P("head"),
            P(None, "head"),
        ),
        out_specs=P(None, "ctx", "head"),
        check_vma=False,
    )
```

profile of v0, /device:TPU:0, one launch (start us, length us, event | category | flops | bytes accessed | tf_op | source)
XLA Modules:
  0.0 567.8 jit_solution(12068250197391471740)
XLA Ops:
  27.0 43.1 %all-gather.1 = bf16[16,8,1,1]{1,3,2,0:T(2,128)(2,1)S(1)} all-gather(bf16[1,8,1,1]{1,3,2,0:T(2,128)(2,1)S(1)} %copy.158), channel_id=3, replica_groups=mesh['ctx'=16,'head'=2] {'ctx'}, dimensions={0}, use_global_device_ids=true | all-gather | bytes 272 | tf_op jit(solution)/shard_map/all_gather | solution.py:43
  70.2 36.6 %all-gather = f32[16,8,1,1]{1,3,2,0:T(1,128)S(1)} all-gather(f32[1,8,1,1]{1,3,2,0:T(1,128)S(1)} %copy.137), channel_id=2, replica_groups=mesh['ctx'=16,'head'=2] {'ctx'}, dimensions={0}, use_global_device_ids=true | all-gather | bytes 544 | tf_op jit(solution)/shard_map/all_gather | solution.py:17
  113.4 18.8 %all-gather.10.cloned.1.call-done = f32[16,8,128,128]{3,2,1,0:T(8,128)} async-done(((f32[1,8,128,128]{3,2,1,0:T(8,128)}), f32[16,8,128,128]{3,2,1,0:T(8,128)}) %all-gather.10.cloned.1.call-update) | async-done | bytes 8388624 | tf_op jit(solution)/shard_map/all_gather | solution.py:17
  132.2 113.3 %all-gather.8.cloned.1.call-done = f32[16,8,128,128]{3,2,1,0:T(8,128)} async-done(((f32[1,8,128,128]{3,2,1,0:T(8,128)}), f32[16,8,128,128]{3,2,1,0:T(8,128)}) %all-gather.8.cloned.1.call-update) | async-done | bytes 8388624 | tf_op jit(solution)/shard_map/all_gather | solution.py:17
  245.6 41.3 %while.33 = (s32[]{:T(128)}, f32[8,128,128]{2,1,0:T(8,128)}, f32[8,128,128]{2,1,0:T(8,128)}, s32[]{:T(128)}, f32[16,8]{1,0:T(8,128)S(1)}, /*index=5*/f32[16,8,12...) while((s32[]{:T(128)}, f32[8,128,128]{2,1,0:T(8,128)}, ...), condition=%wide.region_4.5_spmd.clone, body=%wide.region_3.4_spmd.clone.sunk | while | flops 1048580 | bytes 3145945 | solution.py:26
  248.0 2.8 fusion.128
  250.8 2.8 fusion.128
  253.6 2.8 fusion.128
  259.2 2.8 fusion.128
  262.0 2.8 fusion.128
  264.7 2.8 fusion.128
  267.5 2.8 fusion.128
  273.0 2.8 fusion.128
  275.8 2.8 fusion.128
  281.4 2.8 fusion.128
  284.1 2.8 fusion.128
  289.5 32.6 %all-gather.14.cloned.1.call-done = bf16[16,8,128,128]{3,2,1,0:T(8,128)(2,1)} async-done(((bf16[1,8,128,128]{3,2,1,0:T(8,128)(2,1)}), bf16[16,8,128,128]{3,2,1,0:T(8,128)(2,1)}) %all-gather.14.cloned.1.call-update) | async-done | bytes 4194320 | tf_op jit(solution)/shard_map/all_gather | solution.py:43
  322.1 76.8 %all-gather.12.cloned.1.call-done = bf16[16,8,128,128]{3,2,1,0:T(8,128)(2,1)} async-done(((bf16[1,8,128,128]{3,2,1,0:T(8,128)(2,1)}), bf16[16,8,128,128]{3,2,1,0:T(8,128)(2,1)}) %all-gather.12.cloned.1.call-update) | async-done | bytes 4194320 | tf_op jit(solution)/shard_map/all_gather | solution.py:43
  400.7 38.6 %while.32 = (s32[]{:T(128)}, f32[8]{0:T(128)S(1)}, f32[8,128,128]{2,1,0:T(8,128)}, f32[8,128,128]{2,1,0:T(8,128)}, s32[]{:T(128)}, /*index=5*/bf16[16,8]{1,0:T(8...) while((s32[]{:T(128)}, f32[8]{0:T(128)S(1)}, ...), condition=%wide.region_11.12_spmd, body=%wide.region_10.11_spmd.sunk | while | flops 786454 | bytes 2621755 | solution.py:60
  439.3 2.8 fusion.71
  442.2 69.8 %all-reduce.3.cloned.1.call-done = (bf16[8,128,128]{2,1,0:T(8,128)(2,1)}, bf16[8,128,128]{2,1,0:T(8,128)(2,1)}) async-done(((bf16[8,128,128]{2,1,0:T(8,128)(2,1)}, bf16[8,128,128]{2,1,0:T(8,128)(2,1)}), (bf16[8,128,128]{2,1,0:T(8,128)(2,1)}, bf16[8,128,128]{2,1,0:T(8,128)(2,1)})) %all-reduce.3.cloned.1.call-update) | async-done | bytes 524304 | tf_op jit(solution)/shard_map/psum | solution.py:35
  514.2 2.9 fusion.49
  541.3 9.8 %all-gather.16.cloned.1.call-done = bf16[512,2048]{0,1:T(8,128)(2,1)} async-done(((bf16[512,1024]{0,1:T(8,128)(2,1)}), bf16[512,2048]{0,1:T(8,128)(2,1)}) %all-gather.16.cloned.1.call-update) | async-done | bytes 2097168 | tf_op jit(solution)/shard_map/all_gather | solution.py:193
  551.0 9.9 %convolution_convert_fusion = bf16[512,2048]{1,0:T(8,128)(2,1)} fusion(bf16[512,2048]{0,1:T(8,128)(2,1)} %all-gather.16.cloned.1.call-done, bf16[2048,2048]{1,0:T(8,128)(2,1)} %param.17), kind=kOutput, calls=%fused_computation.15 | convolution fusion | flops 4296015872 | bytes 12582912 | tf_op jit(solution)/shard_map/dot_general | solution.py:192
  (163 shorter events, 106.8 us)
Async XLA Ops:
  6.5 125.7 %all-gather.10.cloned.1.call-start = ((), (), s32[]{:S(2)}) async-start(), calls=%async_computation.1 | async-start | bytes 8912896 | tf_op jit(solution)/shard_map/all_gather | solution.py:17
  13.3 3.6 copy-start.6
  16.0 4.7 copy-start.10
  16.9 228.6 %all-gather.8.cloned.1.call-start = ((), (), s32[]{:S(2)}) async-start(), calls=%async_computation | async-start | bytes 8912896 | tf_op jit(solution)/shard_map/all_gather | solution.py:17
  19.7 4.1 copy-start.11
  20.6 301.5 %all-gather.14.cloned.1.call-start = ((), (), s32[]{:S(2)}) async-start(), calls=%async_computation.3 | async-start | bytes 4456448 | tf_op jit(solution)/shard_map/all_gather | solution.py:43
  21.4 377.6 %all-gather.12.cloned.1.call-start = ((), (), s32[]{:S(2)}) async-start(), calls=%async_computation.2 | async-start | bytes 4456448 | tf_op jit(solution)/shard_map/all_gather | solution.py:43
  22.2 489.7 %all-reduce.3.cloned.1.call-start = ((), (), s32[]{:S(2)}) async-start(), calls=%async_computation.5 | async-start | bytes 1048576 | tf_op jit(solution)/shard_map/psum | solution.py:35
  27.0 80.5 %copy-start.5 = (bf16[2,1,256,8,128]{4,2,3,1,0:T(8,128)(2,1)S(1)}, bf16[2,1,256,8,128]{4,2,3,1,0:T(8,128)(2,1)}, u32[]{:S(2)}) copy-start(bf16[2,1,256,8,128]{4,2,3,1,0:T(8,128)(2,1)} %copy.136) | copy-start | bytes 3145732
  289.5 261.6 %all-gather.16.cloned.1.call-start = ((), (), s32[]{:S(2)}) async-start(), calls=%async_computation.4 | async-start | bytes 3145728 | tf_op jit(solution)/shard_map/all_gather | solution.py:193
  439.3 74.8 %copy-start.15 = (f32[8]{0:T(128)S(1)}, f32[8]{0:T(128)}, u32[]{:S(2)}) copy-start(f32[8]{0:T(128)} %param.15) | copy-start | bytes 100
  512.0 2.1 copy-start.9
  514.1 3.0 copy-start
  514.2 3.5 copy-start.8
  514.2 3.7 copy-start.12
  520.7 1.3 copy-start.1
  520.7 1.3 copy-start.13
  524.1 1.0 copy-start.2
  527.6 1.6 copy-start.4
  532.5 1.6 copy-start.3
  532.5 1.6 copy-start.14
  534.1 2.4 copy-start.7
  537.8 1.3 copy-start.16
Sparse Core Ops, SparseCore 0:
  17.1 115.1 all-gather.9
  135.0 110.5 all-gather.7
  248.3 73.7 all-gather.13
  324.7 74.1 all-gather.11
  404.0 107.9 all-reduce.2
  541.4 9.6 all-gather.15
where the time goes:
time: 569 us; the launch traced here: 568 us
  waiting for transfers between devices  321 us (56%)
  other arithmetic  92.9 us (16%)
  blocking collectives  79.7 us (14%)
  matrix products  44.7 us (8%)
  local copies, waits for them, and re-layouts  14.9 us (3%)
  between operations  14 us (2%)
    all_gather x2, waiting for transfers between devices, entering_2(): pieces = jax.tree.map(lambda part: lax.all_gather(part, axis), value)  132 us
    all_gather x2, waiting for transfers between devices, carried_in(): lax.all_gather(a.astype(kind), axis)  109 us
    psum x1, waiting for transfers between devices, broadcast(): return lax.psum(jnp.where(mine, shard, jnp.zeros_like(shard)), axis)  69.8 us
    all_gather x1, blocking collectives, carried_in(): lax.all_gather(a.astype(kind), axis)  43.1 us
    select_n x15, other arithmetic, lap(): jnp.where(position < mine, new, old)  41.1 us
    add x15, other arithmetic, combine(): fading * earlier[2] + latter[2]  38.4 us
    all_gather x1, blocking collectives, entering_2(): pieces = jax.tree.map(lambda part: lax.all_gather(part, axis), value)  36.6 us
  transfers between devices with their start and end apart: 6, of which 6 were waited for; matrix products, arithmetic and copies ran while one was open for 18% of the time, Pallas kernels for 0%

commit v1 on v0

--- a/solution.py
+++ b/solution.py
@@ -32,7 +32,7 @@
 
 def broadcast(shard, axis, root):
     mine = lax.axis_index(axis) == root
-    return lax.psum(jnp.where(mine, shard, jnp.zeros_like(shard)), axis)
+    return jnp.sum(lax.all_gather(jnp.where(mine, shard, jnp.zeros_like(shard)), axis), axis=0)
 
 
 def carried_in(shard, axis, join, neutral):

time: 569 us -> 593 us (1.042)
  waiting for transfers between devices: 321 us -> 351 us
  other arithmetic: 92.9 us -> 79.9 us
    all_gather x0 -> x2, waiting for transfers between devices: none -> 83.3 us  [broadcast(): lax.all_gather(jnp.where(mine, shard, jnp.zeros_like(shard)), axis)]
    psum x1 -> x0, waiting for transfers between devices: 69.8 us -> none  [broadcast(): return lax.psum(jnp.where(mine, shard, jnp.zeros_like(shard)), axis)]
    all_gather x2, waiting for transfers between devices: 132 us -> 180 us  [entering_2(): pieces = jax.tree.map(lambda part: lax.all_gather(part, axis), value)]
    all_gather x2, waiting for transfers between devices: 109 us -> 78.1 us  [carried_in(): lax.all_gather(a.astype(kind), axis)]
    select_n x15, other arithmetic: 41.1 us -> 22.2 us  [lap(): jnp.where(position < mine, new, old)]
    all_gather x1, blocking collectives: 36.6 us -> 43.2 us  [entering_2(): pieces = jax.tree.map(lambda part: lax.all_gather(part, axis), value)]
    reduce_sum x0 -> x2, other arithmetic: none -> 6.04 us  [broadcast(): jnp.sum(lax.all_gather(jnp.where(mine, shard, jnp.zeros_like(shard)), axi...]
  transfers between devices with their start and end apart: 6 -> 7, of which waited for: 6 -> 7; matrix products, arithmetic and copies ran while one was open for 18% -> 19% of each run, Pallas kernels for 0% -> 0%
where the time goes in v1:
time: 593 us; the launch traced here: 592 us
  waiting for transfers between devices  351 us (59%)
  blocking collectives  81.7 us (14%)
  other arithmetic  79.9 us (13%)
  matrix products  49.6 us (8%)
  local copies, waits for them, and re-layouts  15.2 us (3%)
  between operations  14 us (2%)
    all_gather x2, waiting for transfers between devices, entering_2(): pieces = jax.tree.map(lambda part: lax.all_gather(part, axis), value)  180 us
    all_gather x2, waiting for transfers between devices, broadcast(): lax.all_gather(jnp.where(mine, shard, jnp.zeros_like(shard)), axis)  83.3 us
    all_gather x2, waiting for transfers between devices, carried_in(): lax.all_gather(a.astype(kind), axis)  78.1 us
    all_gather x1, blocking collectives, entering_2(): pieces = jax.tree.map(lambda part: lax.all_gather(part, axis), value)  43.2 us
    all_gather x1, blocking collectives, carried_in(): lax.all_gather(a.astype(kind), axis)  38.6 us
    add x15, other arithmetic, combine(): fading * earlier[2] + latter[2]  38.5 us
    select_n x15, other arithmetic, lap(): jnp.where(position < mine, new, old)  22.2 us
  transfers between devices with their start and end apart: 7, of which 7 were waited for; matrix products, arithmetic and copies ran while one was open for 19% of the time, Pallas kernels for 0%

profile of v1, /device:TPU:0, one launch (start us, length us, event | category | flops | bytes accessed | tf_op | source)
XLA Modules:
  0.0 591.8 jit_solution(10801368998767087110)
XLA Ops:
  13.3 2.7 fusion.67
  16.9 2.7 fusion.64
  22.5 43.2 %all-gather = f32[16,8,1,1]{1,3,2,0:T(1,128)S(1)} all-gather(f32[1,8,1,1]{1,3,2,0:T(1,128)S(1)} %copy.137), channel_id=2, replica_groups=mesh['ctx'=16,'head'=2] {'ctx'}, dimensions={0}, use_global_device_ids=true | all-gather | bytes 544 | tf_op jit(solution)/shard_map/all_gather | solution.py:17
  65.7 66.4 %all-gather.14.cloned.1.call-done = f32[16,8,128,128]{3,2,1,0:T(8,128)} async-done(((f32[1,8,128,128]{3,2,1,0:T(8,128)}), f32[16,8,128,128]{3,2,1,0:T(8,128)}) %all-gather.14.cloned.1.call-update) | async-done | bytes 8388624 | tf_op jit(solution)/shard_map/all_gather | solution.py:17
  132.1 113.3 %all-gather.12.cloned.1.call-done = f32[16,8,128,128]{3,2,1,0:T(8,128)} async-done(((f32[1,8,128,128]{3,2,1,0:T(8,128)}), f32[16,8,128,128]{3,2,1,0:T(8,128)}) %all-gather.12.cloned.1.call-update) | async-done | bytes 8388624 | tf_op jit(solution)/shard_map/all_gather | solution.py:17
  245.3 22.8 %while.33 = (s32[]{:T(128)}, f32[8,128,128]{2,1,0:T(8,128)S(1)}, f32[8,128,128]{2,1,0:T(8,128)S(1)}, s32[]{:T(128)}, f32[16,8]{1,0:T(8,128)S(1)}, /*index=5*/f32...) while((s32[]{:T(128)}, f32[8,128,128]{2,1,0:T(8,128)S(1)}, ...), condition=%wide.region_4.5_spmd.clone, body=%wide.region_3.4_spmd.clone.sunk | while | flops 1048580 | bytes 3145945 | solution.py:26
  270.9 38.6 %all-gather.1 = bf16[16,8,1,1]{1,3,2,0:T(2,128)(2,1)S(1)} all-gather(bf16[1,8,1,1]{1,3,2,0:T(2,128)(2,1)S(1)} %copy.158), channel_id=3, replica_groups=mesh['ctx'=16,'head'=2] {'ctx'}, dimensions={0}, use_global_device_ids=true | all-gather | bytes 272 | tf_op jit(solution)/shard_map/all_gather | solution.py:43
  321.9 76.9 %all-gather.16.cloned.1.call-done = bf16[16,8,128,128]{3,2,1,0:T(8,128)(2,1)} async-done(((bf16[1,8,128,128]{3,2,1,0:T(8,128)(2,1)}), bf16[16,8,128,128]{3,2,1,0:T(8,128)(2,1)}) %all-gather.16.cloned.1.call-update) | async-done | bytes 4194320 | tf_op jit(solution)/shard_map/all_gather | solution.py:43
  400.5 38.7 %while.32 = (s32[]{:T(128)}, f32[8]{0:T(128)S(1)}, f32[8,128,128]{2,1,0:T(8,128)}, f32[8,128,128]{2,1,0:T(8,128)}, s32[]{:T(128)}, /*index=5*/bf16[16,8]{1,0:T(8...) while((s32[]{:T(128)}, f32[8]{0:T(128)S(1)}, ...), condition=%wide.region_11.12_spmd, body=%wide.region_10.11_spmd.sunk | while | flops 786454 | bytes 2621755 | solution.py:60
  405.7 2.6 convert_add_fusion.3
  408.3 2.6 convert_add_fusion.3
  413.4 2.6 convert_add_fusion.3
  431.5 2.6 convert_add_fusion.3
  436.6 2.6 convert_add_fusion.3
  439.2 2.8 fusion.71
  442.0 33.6 %all-gather.22.cloned.1.call-done = bf16[128,128,128]{2,1,0:T(8,128)(2,1)} async-done(((bf16[8,128,128]{2,1,0:T(8,128)(2,1)}), bf16[128,128,128]{2,1,0:T(8,128)(2,1)}) %all-gather.22.cloned.1.call-update) | async-done | bytes 4194320 | tf_op jit(solution)/shard_map/all_gather | solution.py:35
  475.6 3.0 reduce_sum.120
  480.8 2.9 fusion.49
  502.8 49.7 %all-gather.24.cloned.1.call-done = bf16[128,128,128]{2,1,0:T(8,128)(2,1)} async-done(((bf16[8,128,128]{2,1,0:T(8,128)(2,1)}), bf16[128,128,128]{2,1,0:T(8,128)(2,1)}) %all-gather.24.cloned.1.call-update) | async-done | bytes 4194320 | tf_op jit(solution)/shard_map/all_gather | solution.py:35
  552.5 3.1 reduce_sum.124
  555.6 3.0 convolution_multiply_fusion
  558.7 3.1 multiply_reduce_fusion
  565.7 9.3 %all-gather.20.cloned.1.call-done = bf16[512,2048]{0,1:T(8,128)(2,1)} async-done(((bf16[512,1024]{0,1:T(8,128)(2,1)}), bf16[512,2048]{0,1:T(8,128)(2,1)}) %all-gather.20.cloned.1.call-update) | async-done | bytes 2097168 | tf_op jit(solution)/shard_map/all_gather | solution.py:193
  575.1 9.9 %convolution_convert_fusion = bf16[512,2048]{1,0:T(8,128)(2,1)} fusion(bf16[512,2048]{0,1:T(8,128)(2,1)} %all-gather.20.cloned.1.call-done, bf16[2048,2048]{1,0:T(8,128)(2,1)} %param.17), kind=kOutput, calls=%fused_computation.15 | convolution fusion | flops 4296015872 | bytes 12582912 | tf_op jit(solution)/shard_map/dot_general | solution.py:192
  (176 shorter events, 100.3 us)
Async XLA Ops:
  6.5 125.5 %all-gather.14.cloned.1.call-start = ((), (), s32[]{:S(2)}) async-start(), calls=%async_computation.1 | async-start | bytes 8912896 | tf_op jit(solution)/shard_map/all_gather | solution.py:17
  13.3 3.5 copy-start.10
  16.9 228.5 %all-gather.12.cloned.1.call-start = ((), (), s32[]{:S(2)}) async-start(), calls=%async_computation | async-start | bytes 8912896 | tf_op jit(solution)/shard_map/all_gather | solution.py:17
  19.6 2.6 copy-start.16
  20.5 301.4 %all-gather.18.cloned.1.call-start = ((), (), s32[]{:S(2)}) async-start(), calls=%async_computation.3 | async-start | bytes 4456448 | tf_op jit(solution)/shard_map/all_gather | solution.py:43
  21.3 377.5 %all-gather.16.cloned.1.call-start = ((), (), s32[]{:S(2)}) async-start(), calls=%async_computation.2 | async-start | bytes 4456448 | tf_op jit(solution)/shard_map/all_gather | solution.py:43
  22.2 453.5 %all-gather.22.cloned.1.call-start = ((), (), s32[]{:S(2)}) async-start(), calls=%async_computation.5 | async-start | bytes 4456448 | tf_op jit(solution)/shard_map/all_gather | solution.py:35
  268.2 42.7 %copy-start.5 = (f32[8,128,128]{2,1,0:T(8,128)}, f32[8,128,128]{2,1,0:T(8,128)S(1)}, u32[]{:S(2)}) copy-start(f32[8,128,128]{2,1,0:T(8,128)S(1)} %get-tuple-element.236) | copy-start | bytes 1572868
  268.2 42.7 %copy-start.7 = (f32[8,128,128]{2,1,0:T(8,128)}, f32[8,128,128]{2,1,0:T(8,128)S(1)}, u32[]{:S(2)}) copy-start(f32[8,128,128]{2,1,0:T(8,128)S(1)} %get-tuple-element.237) | copy-start | bytes 1572868
  270.7 281.8 %all-gather.24.cloned.1.call-start = ((), (), s32[]{:S(2)}) async-start(), calls=%async_computation.6 | async-start | bytes 4456448 | tf_op jit(solution)/shard_map/all_gather | solution.py:35
  312.3 2.2 copy-start.9
  320.6 254.4 %all-gather.20.cloned.1.call-start = ((), (), s32[]{:S(2)}) async-start(), calls=%async_computation.4 | async-start | bytes 3145728 | tf_op jit(solution)/shard_map/all_gather | solution.py:193
  478.6 2.1 copy-start.13
  478.6 2.1 copy-start.19
  480.7 3.0 copy-start
  480.7 3.5 copy-start.12
  480.8 3.7 copy-start.17
  488.4 11.9 %copy-start.2 = (f32[8,256,128]{2,1,0:T(8,128)}, f32[8,256,128]{2,1,0:T(8,128)S(1)}, u32[]{:S(2)}) copy-start(f32[8,256,128]{2,1,0:T(8,128)S(1)} %get-tuple-element.387) | copy-start | bytes 3145732
  552.5 3.1 copy-start.3
  555.6 3.1 copy-start.11
  555.6 3.1 copy-start.15
  555.6 6.2 %copy-start.18 = (f32[8,256,128]{2,1,0:T(8,128)S(1)}, f32[8,256,128]{2,1,0:T(8,128)}, u32[]{:S(2)}) copy-start(f32[8,256,128]{2,1,0:T(8,128)} %convolution_multiply_fusion.3) | copy-start | bytes 3145732
  558.7 3.1 copy-start.1
  558.7 3.5 copy-start.14
  (4 other events, 5.2 us)
Sparse Core Ops, SparseCore 0:
  17.0 115.0 all-gather.13
  134.8 110.4 all-gather.11
  248.1 73.7 all-gather.17
  324.6 74.1 all-gather.15
  401.4 74.1 all-gather.21
  478.3 74.1 all-gather.23
  565.9 9.1 all-gather.19
